TPU v7x, 128 devices: a whole 4x4x4 slice. The times are simulated.
128 devices in a mesh: section: 4 (over z), row: 8 (over x, core), col: 4 (over y).
Axes of the slice: x: 4, y: 4, z: 4, core: 2. Of those that a mesh axis runs over, the one named last changes fastest.
Arguments:
- tokens: bfloat16 [4, 512, 4096], P('section', 'col', 'row'), may hold values from -6 to 6
- cotangent: bfloat16 [4, 512, 4096], P('section', 'col', 'row'), may hold values from -6 to 6
- noised: int32 [4, 512], P('section', 'col'), may hold values from 0 to 1, as said below
- gate_weight: bfloat16 [4, 4096, 16384], P('section', None, ('row', 'col')), may hold values from -0.09375 to 0.09375
- up_weight: bfloat16 [4, 4096, 16384], P('section', None, ('row', 'col')), may hold values from -0.09375 to 0.09375
- down_weight: bfloat16 [4, 16384, 4096], P('section', ('row', 'col')), may hold values from -0.046875 to 0.046875
- block_keep: int32 [4, 3, 32, 128], P('section', None, None, ('row', 'col')), may hold values 0 or 1
Outputs:
- grad_gate: bfloat16 [4, 4096, 16384], P('section', None, ('row', 'col'))
- grad_up: bfloat16 [4, 4096, 16384], P('section', None, ('row', 'col'))
- grad_down: bfloat16 [4, 16384, 4096], P('section', ('row', 'col'))
- handoff: bfloat16 [4, 512, 4096], P('section', 'col')
Inputs may be any that keep to these rules, and one draw needn't show every extreme that they name: Each aligned block of 128 tokens of a section (the tokens of one grid column) holds 1 to 96 noised tokens; in every section some block holds exactly 96.
All inputs are finite; a program needn't handle non-finite values. No bound on the sum of `block_keep` on one device may be relied on, other than what follows from the above.
Results may differ from a plain program's by a relative error of at most 0.0051.
Values may be sent and summed in bfloat16 or wider, within the bound.
No kernel may reach another device: no remote copies, remote signals or barrier semaphores. Data moves between devices by JAX's collectives and lax.ppermute only.
A program may use at most 128 MiB of HBM per device.

v0:
```python
import jax
import jax.numpy as jnp
from jax import lax
from jax.sharding import PartitionSpec as P


def shifted(array, axis, by):
    peers = lax.axis_size(axis)
    pairs = [(i, i + by) for i in range(peers) if 0 <= i + by < peers]
    return lax.ppermute(array, axis, pairs)


def expand_blocks(block_mask, block_edge):
    widened = jnp.repeat(jnp.repeat(block_mask, block_edge, axis=0), block_edge, axis=1)
    return widened.astype(jnp.bfloat16)


def contract_rows(left, right):
    return lax.dot_general(
        left, right, (((0,), (0,)), ((), ())), preferred_element_type=jnp.float32
    )


def contract_cols(left, right):
    return lax.dot_general(
        left, right, (((1,), (1,)), ((), ())), preferred_element_type=jnp.float32
    )


def on_device(tokens, cotangent, noised, gate_weight, up_weight, down_weight, block_keep):
    local_tokens = tokens[0]
    local_noised = noised[0]
    gate_mask = expand_blocks(block_keep[0, 0], 128)
    up_mask = expand_blocks(block_keep[0, 1], 128)
    down_mask = expand_blocks(block_keep[0, 2].T, 128)
    gate_eff = gate_weight[0] * gate_mask
    up_eff = up_weight[0] * up_mask
    down_eff = down_weight[0] * down_mask
    masked_cot = cotangent[0] * local_noised[:, None].astype(jnp.bfloat16)
    row_count = lax.axis_size("row")
    per_row = local_tokens.shape[0] // row_count

    def regroup(block):
        return block.reshape(row_count, per_row, block.shape[1])

    def flatten(block):
        return block.reshape(block.shape[0] * block.shape[1], block.shape[2])

    wide_tokens, wide_cot = (
        lax.all_gather(local_tokens, "row", axis=1, tiled=True),
        lax.all_gather(masked_cot, "row", axis=1, tiled=True),
    )
    grouped_tokens, grouped_cot = (
        lax.all_gather(regroup(wide_tokens), "col", axis=1, tiled=True),
        lax.all_gather(regroup(wide_cot), "col", axis=1, tiled=True),
    )
    gathered_tokens = flatten(grouped_tokens)
    gathered_cot = flatten(grouped_cot)
    gate_pre = jnp.dot(gathered_tokens, gate_eff, preferred_element_type=jnp.float32)
    up_pre = jnp.dot(gathered_tokens, up_eff, preferred_element_type=jnp.float32)
    sigmoid_gate = jax.nn.sigmoid(gate_pre)
    silu_gate = gate_pre * sigmoid_gate
    hidden = (silu_gate * up_pre).astype(jnp.bfloat16)
    grad_hidden = contract_cols(gathered_cot, down_eff)
    grad_down = (contract_rows(hidden, gathered_cot) * down_mask).astype(jnp.bfloat16)
    grad_gate_pre = (
        grad_hidden * up_pre * sigmoid_gate * (1.0 + gate_pre * (1.0 - sigmoid_gate))
    ).astype(jnp.bfloat16)
    grad_up_pre = (grad_hidden * silu_gate).astype(jnp.bfloat16)
    grad_gate = (contract_rows(gathered_tokens, grad_gate_pre) * gate_mask).astype(jnp.bfloat16)
    grad_up = (contract_rows(gathered_tokens, grad_up_pre) * up_mask).astype(jnp.bfloat16)
    summed_rows = lax.psum_scatter(
        contract_cols(grad_gate_pre, gate_eff) + contract_cols(grad_up_pre, up_eff),
        ("row", "col"),
        scatter_dimension=0,
        tiled=True,
    )
    share_rows = summed_rows.astype(jnp.bfloat16)
    column_block = lax.all_gather(share_rows, "row", axis=0, tiled=True)
    handoff = shifted(column_block, "section", -1)
    return (grad_gate[None], grad_up[None], grad_down[None], handoff[None])


def solution(mesh):
    placed = (
        P("section", "col", "row"),
        P("section", "col", "row"),
        P("section", "col"),
        P("section", None, ("row", "col")),
        P("section", None, ("row", "col")),
        P("section", ("row", "col"), None),
        P("section", None, None, ("row", "col")),
    )
    return jax.shard_map(
        on_device,
        mesh=mesh,
        in_specs=placed,
        out_specs=(
            P("section", None, ("row", "col")),
            P("section", None, ("row", "col")),
            P("section", ("row", "col"), None),
            P("section", "col", None),
        ),
        check_vma=False,
    )
```

profile of v0, /device:TPU:97, one launch (start us, length us, event | category | flops | bytes accessed | tf_op | source)
XLA Modules:
  0.0 337.1 jit_solution(13740636313330585911)
XLA Ops:
  8.6 1.6 bitcast_multiply_fusion.5
  10.3 24.3 %all-gather.15.cloned.1.call-done = bf16[1,128,4096]{2,1,0:T(8,128)(2,1)} async-done(((bf16[1,128,512]{2,1,0:T(8,128)(2,1)}), bf16[1,128,4096]{2,1,0:T(8,128)(2,1)}) %all-gather.15.cloned.1.call-update) | async-done | bytes 1048592 | tf_op jit(solution)/shard_map/all_gather | solution.py:50
  34.7 25.3 %all-gather.7.cloned.1.call-done = bf16[128,4096]{1,0:T(8,128)(2,1)} async-done(((bf16[128,512]{1,0:T(8,128)(2,1)}), bf16[128,4096]{1,0:T(8,128)(2,1)}) %all-gather.7.cloned.1.call-update) | async-done | bytes 1048592 | tf_op jit(solution)/shard_map/all_gather | solution.py:51
  60.1 0.7 fusion.24
  60.9 2.5 broadcast_in_dim.39
  63.4 6.4 %copy.22 = bf16[1,4096,512]{2,1,0:T(8,128)(2,1)} copy(bf16[1,4096,512]{1,2,0:T(8,128)(2,1)} %bitcast.101) | data formatting | bytes 8388608 | tf_op jit(solution)/shard_map/convert_element_type | solution.py:15
  69.9 2.5 broadcast_in_dim.37
  72.4 6.5 %copy.21 = bf16[1,4096,512]{2,1,0:T(8,128)(2,1)} copy(bf16[1,4096,512]{1,2,0:T(8,128)(2,1)} %bitcast.99) | data formatting | bytes 8388608 | tf_op jit(solution)/shard_map/convert_element_type | solution.py:15
  78.9 3.8 %broadcast_in_dim.35 = bf16[512,32,128]{2,1,0:T(8,128)(2,1)} broadcast(bf16[512,32]{1,0:T(8,128)(2,1)S(1)} %bitcast.113), dimensions={0,1} | broadcast | bytes 4227072 | tf_op jit(solution)/shard_map/broadcast_in_dim | solution.py:14
  82.7 7.4 %convert_element_type.142 = bf16[1,512,4096]{2,1,0:T(8,128)(2,1)} reshape(bf16[512,32,128]{2,1,0:T(8,128)(2,1)} %broadcast_in_dim.35) | data formatting | bytes 8388608 | tf_op jit(solution)/shard_map/convert_element_type | solution.py:15
  90.1 6.4 %copy.15 = bf16[1,4096,512]{1,2,0:T(8,128)(2,1)} copy(bf16[1,4096,512]{2,1,0:T(8,128)(2,1)} %param.10) | data formatting | bytes 8388608 | tf_op args[3]
  96.5 4.4 %bitcast_multiply_fusion.4 = bf16[4096,512]{0,1:T(8,128)(2,1)} fusion(bf16[1,4096,512]{1,2,0:T(8,128)(2,1)} %copy.15, bf16[4096,4]{0,1:T(4,128)(2,1)S(1)} %bitcast.115), kind=kLoop, calls=%fused_computation.7 | loop fusion | flops 2097152 | bytes 8421376 | tf_op jit(solution)/shard_map/mul | solution.py:36
  100.9 6.4 %copy.16 = bf16[1,4096,512]{1,2,0:T(8,128)(2,1)} copy(bf16[1,4096,512]{2,1,0:T(8,128)(2,1)} %param.11) | data formatting | bytes 8388608 | tf_op args[4]
  107.3 4.5 %bitcast_multiply_fusion.3 = bf16[4096,512]{0,1:T(8,128)(2,1)} fusion(bf16[1,4096,512]{1,2,0:T(8,128)(2,1)} %copy.16, bf16[4096,4]{0,1:T(4,128)(2,1)S(1)} %bitcast.117), kind=kLoop, calls=%fused_computation.6 | loop fusion | flops 2097152 | bytes 8421376 | tf_op jit(solution)/shard_map/mul | solution.py:37
  111.8 7.1 %fusion.18 = f32[512,512]{1,0:T(8,128)S(1)} fusion(bf16[512,4096]{1,0:T(8,128)(2,1)} %bitcast.104, bf16[1,4096,512]{2,1,0:T(8,128)(2,1)} %param.10, bf16[1,4096,512]{2,1,0:T(8,128)(2,1)} %copy.22), kind=kOutput, calls=%fused_computation.22 | convolution fusion | flops 2149580800 | bytes 13631488 | tf_op jit(solution)/shard_map/dot_general | solution.py:59
  119.0 1.1 copy-done.4
  120.1 2.3 fusion.15
  122.4 36.9 %all-gather.9.cloned.1.call-done = bf16[8,64,4096]{2,1,0:T(8,128)(2,1)} async-done(((bf16[8,16,4096]{2,1,0:T(8,128)(2,1)}), bf16[8,64,4096]{2,1,0:T(8,128)(2,1)}) %all-gather.9.cloned.1.call-update) | async-done | bytes 4194320 | tf_op jit(solution)/shard_map/all_gather | solution.py:55
  159.3 7.4 %multiply_convert_fusion.1 = (bf16[512,512]{1,0:T(8,128)(2,1)S(1)}, bf16[512,512]{1,0:T(8,128)(2,1)S(1)}) fusion(f32[512,512]{1,0:T(8,128)S(1)} %fusion.18, f32[512,512]{1,0:T(8,128)S(1)} %fusion.15, bf16[512,4096]{1,0:T(8,128)(2,1)} %bitcast.108, bf16[1,512,4096]{2,1,0:T(8,128)(2,1)} %param.12, bf16[1,512,4096]{2,1,0:T(8,128)(2,1)} %convert_element_type.142), kind=kOutput, calls=%fused_computation.24 | convolution fusion | flops 2152988672 | bytes 15728640 | tf_op jit(solution)/shard_map/dot_general | solution.py:25
  166.8 2.3 fusion.27
  169.2 5.6 %convolution_add_fusion = f32[512,4096]{1,0:T(8,128)} fusion(f32[512,4096]{1,0:T(8,128)S(1)} %fusion.27, bf16[512,512]{1,0:T(8,128)(2,1)S(1)} %get-tuple-element.8, bf16[4096,512]{0,1:T(8,128)(2,1)S(1)} %copy-done.2), kind=kOutput, calls=%fused_computation.8 | convolution fusion | flops 2149580800 | bytes 21495808 | tf_op jit(solution)/shard_map/dot_general | solution.py:25
  175.1 91.2 %reduce-scatter.2.cloned.1.call-done = f32[16,4096]{1,0:T(8,128)} async-done(((f32[512,4096]{1,0:T(8,128)}), f32[16,4096]{1,0:T(8,128)}) %reduce-scatter.2.cloned.1.call-update) | async-done | bytes 262160 | tf_op jit(solution)/shard_map/reduce_scatter | solution.py:72
  266.3 1.6 convert_element_type.164
  268.0 7.9 %fusion.3 = bf16[1,4096,512]{1,2,0:T(8,128)(2,1)} fusion(bf16[4096,512]{0,1:T(8,128)(2,1)} %bitcast.102, bf16[512,512]{1,0:T(8,128)(2,1)S(1)} %get-tuple-element.9, bf16[512,4096]{1,0:T(8,128)(2,1)} %bitcast.105), kind=kOutput, calls=%fused_computation.9 | convolution fusion | flops 2153775104 | bytes 13107200 | tf_op jit(solution)/shard_map/dot_general | solution.py:19
  275.8 17.3 %all-gather.13.cloned.1.call-done = bf16[128,4096]{1,0:T(8,128)(2,1)} async-done(((bf16[16,4096]{1,0:T(8,128)(2,1)}), bf16[128,4096]{1,0:T(8,128)(2,1)}) %all-gather.13.cloned.1.call-update) | async-done | bytes 1048592 | tf_op jit(solution)/shard_map/all_gather | solution.py:79
  293.1 3.4 %collective-permute-start = (bf16[128,4096]{1,0:T(8,128)(2,1)}, bf16[128,4096]{1,0:T(8,128)(2,1)}, u32[]{:S(2)}, u32[]{:S(2)}) collective-permute-start(bf16[128,4096]{1,0:T(8,128)(2,1)} %all-gather.13.cloned.1.call-done), channel_id=1, source_target_pairs={{32,0},{64,32},{96,64},{33,1},{65,33},{97,65},{34,2},{66,34},{98,6... | collective-permute-start | bytes 3145736 | tf_op jit(solution)/shard_map/ppermute | solution.py:10
  296.5 7.8 %fusion.4 = bf16[1,4096,512]{1,2,0:T(8,128)(2,1)} fusion(bf16[4096,512]{0,1:T(8,128)(2,1)} %bitcast.100, bf16[512,512]{1,0:T(8,128)(2,1)S(1)} %get-tuple-element.8, bf16[512,4096]{1,0:T(8,128)(2,1)} %bitcast.106), kind=kOutput, calls=%fused_computation.10 | convolution fusion | flops 2153775104 | bytes 13107200 | tf_op jit(solution)/shard_map/dot_general | solution.py:19
  304.3 6.4 %copy.17 = bf16[1,4096,512]{2,1,0:T(8,128)(2,1)} copy(bf16[1,4096,512]{1,2,0:T(8,128)(2,1)} %fusion.3) | data formatting | bytes 8388608
  310.7 6.4 %copy.18 = bf16[1,4096,512]{2,1,0:T(8,128)(2,1)} copy(bf16[1,4096,512]{1,2,0:T(8,128)(2,1)} %fusion.4) | data formatting | bytes 8388608
  317.1 2.3 broadcast_in_dim.43
  319.5 8.5 %fusion.5 = bf16[1,512,4096]{2,1,0:T(8,128)(2,1)} fusion(f32[64,8,32,128]{3,2,1,0:T(8,128)S(1)} %bitcast.103, bf16[512,4096]{1,0:T(8,128)(2,1)S(1)} %bitcast.109, f32[512,512]{1,0:T(8,128)S(1)} %fusion.15, f32[512,512]{1,0:T(8,128)S(1)} %fusion.18), kind=kOutput, calls=%fused_computation.11 | convolution fusion | flops 2153250816 | bytes 18874368 | tf_op jit(solution)/shard_map/dot_general | solution.py:19
  328.0 2.3 copy.34
  (31 shorter events, 2.1 us)
Async XLA Ops:
  7.2 27.4 %all-gather.15.cloned.1.call-start = ((), (), s32[]{:S(2)}) async-start(), calls=%async_computation.6 | async-start | bytes 1179648 | tf_op jit(solution)/shard_map/all_gather | solution.py:50
  7.9 52.1 %all-gather.7.cloned.1.call-start = ((), (), s32[]{:S(2)}) async-start(), calls=%async_computation.1 | async-start | bytes 1179648 | tf_op jit(solution)/shard_map/all_gather | solution.py:51
  10.3 101.5 %all-gather.11.cloned.1.call-start = ((), (), s32[]{:S(2)}) async-start(), calls=%async_computation.3 | async-start | bytes 5242880 | tf_op jit(solution)/shard_map/all_gather | solution.py:54
  34.6 124.7 %all-gather.9.cloned.1.call-start = ((), (), s32[]{:S(2)}) async-start(), calls=%async_computation.2 | async-start | bytes 5242880 | tf_op jit(solution)/shard_map/all_gather | solution.py:55
  60.0 206.3 %reduce-scatter.2.cloned.1.call-start = ((), (), s32[]{:S(2)}) async-start(), calls=%async_computation.4 | async-start | bytes 8650752 | tf_op jit(solution)/shard_map/reduce_scatter | solution.py:72
  111.8 7.1 %copy-start = (bf16[8,64,4096]{2,1,0:T(8,128)(2,1)S(1)}, bf16[8,64,4096]{2,1,0:T(8,128)(2,1)}, u32[]{:S(2)}) copy-start(bf16[8,64,4096]{2,1,0:T(8,128)(2,1)} %all-gather.11.cloned.1.call-done) | copy-start | bytes 12582916
  111.8 7.1 %copy-start.3 = (bf16[1,4096,512]{2,1,0:T(8,128)(2,1)S(1)}, bf16[1,4096,512]{2,1,0:T(8,128)(2,1)}, u32[]{:S(2)}) copy-start(bf16[1,4096,512]{2,1,0:T(8,128)(2,1)} %param.11) | copy-start | bytes 12582916
  111.8 8.3 %copy-start.4 = (bf16[1,4096,512]{2,1,0:T(8,128)(2,1)S(1)}, bf16[1,4096,512]{2,1,0:T(8,128)(2,1)}, u32[]{:S(2)}) copy-start(bf16[1,4096,512]{2,1,0:T(8,128)(2,1)} %copy.21) | copy-start | bytes 12582916
  159.3 7.5 %copy-start.1 = (bf16[4096,512]{0,1:T(8,128)(2,1)S(1)}, bf16[4096,512]{0,1:T(8,128)(2,1)}, u32[]{:S(2)}) copy-start(bf16[4096,512]{0,1:T(8,128)(2,1)} %bitcast_multiply_fusion.4) | copy-start | bytes 12582916
  166.8 2.4 copy-start.2
  174.8 118.3 %all-gather.13.cloned.1.call-start = ((), (), s32[]{:S(2)}) async-start(), calls=%async_computation.5 | async-start | bytes 1179648 | tf_op jit(solution)/shard_map/all_gather | solution.py:79
  293.1 34.9 %collective-permute-start = (bf16[128,4096]{1,0:T(8,128)(2,1)}, bf16[128,4096]{1,0:T(8,128)(2,1)}, u32[]{:S(2)}, u32[]{:S(2)}) collective-permute-start(bf16[128,4096]{1,0:T(8,128)(2,1)} %all-gather.13.cloned.1.call-done), channel_id=1, source_target_pairs={{32,0},{64,32},{96,64},{33,1},{65,33},{97,65},{34,2},{66,34},{98,6... | collective-permute-start | bytes 3145736 | tf_op jit(solution)/shard_map/ppermute | solution.py:10
  317.1 2.3 copy-start.5
Sparse Core Ops, SparseCore 0:
  9.7 24.8 all-gather.14
  36.9 23.0 all-gather.6
  61.7 47.5 all-gather.10
  110.7 48.5 all-gather.8
  174.9 91.3 reduce-scatter.1
  268.5 24.6 all-gather.12
where the time goes:
time: 338 us; the launch traced here: 337 us
  waiting for transfers between devices  196 us (58%)
  local copies, waits for them, and re-layouts  60.7 us (18%)
  matrix products  49.1 us (15%)
  between operations  14.2 us (4%)
  other arithmetic  13.6 us (4%)
  starting transfers between devices  3.83 us (1%)
    reduce_scatter x1, waiting for transfers between devices, on_device(): lax.psum_scatter(contract_cols(grad_gate_pre, gate_eff) + contract_cols(g...  91.2 us
    all_gather x1, waiting for transfers between devices, on_device(): lax.all_gather(regroup(wide_cot), 'col', axis=1, tiled=True)  36.9 us
    unnamed x20, local copies, waits for them, and re-layouts  29.2 us
    all_gather x1, waiting for transfers between devices, on_device(): lax.all_gather(masked_cot, 'row', axis=1, tiled=True)  25.3 us
    all_gather x1, waiting for transfers between devices, on_device(): lax.all_gather(local_tokens, 'row', axis=1, tiled=True)  24.3 us
    dot_general x3, matrix products, contract_rows(): lax.dot_general(left, right, (((0,), (0,)), ((), ())), preferred_element_...  24.2 us
    convert_element_type x3, local copies, waits for them, and re-layouts, expand_blocks(): return widened.astype(jnp.bfloat16)  20.3 us
    all_gather x1, waiting for transfers between devices, on_device(): column_block = lax.all_gather(share_rows, 'row', axis=0, tiled=True)  17.3 us
  transfers between devices with their start and end apart: 7, of which 5 were waited for; matrix products, arithmetic and copies ran while one was open for 30% of the time, Pallas kernels for 0%

commit v1 on v0

v1 whole, which is shorter than its diff:
```python
import jax
import jax.numpy as jnp
from jax import lax
from jax.experimental import pallas as pl
from jax.experimental.pallas import tpu as pltpu
from jax.sharding import PartitionSpec as P


BF = jnp.bfloat16
F32 = jnp.float32
CAP = 96
SHIFTS = (0, 1, -1, 2)
ANY = pl.BlockSpec(memory_space=pl.ANY)
VM = pl.BlockSpec(memory_space=pltpu.VMEM)


def cost(flops, nbytes):
    return pl.CostEstimate(flops=int(flops), bytes_accessed=int(nbytes), transcendentals=0)


def phase(array, which, by):
    pairs = []
    for x in range(4):
        for core in range(2):
            for y in range(4):
                along_x = (core == 0) == (which == 0)
                tx, ty = ((x + by) % 4, y) if along_x else (x, (y + by) % 4)
                pairs.append(((x * 2 + core) * 4 + y, (tx * 2 + core) * 4 + ty))
    return lax.ppermute(array, ("row", "col"), pairs)


def swap_cores(array):
    return lax.ppermute(array, "row", [(i, i ^ 1) for i in range(8)])


def along_x(array, by):
    return lax.ppermute(array, "row", [(i, (i + 2 * by) % 8) for i in range(8)])


def to_preceding(array):
    return lax.ppermute(array, "section", [(i, i - 1) for i in range(1, 4)])


def selector(noised):
    flags = noised.astype(F32)
    lower = lax.broadcasted_iota(jnp.int32, (128, 128), 0) <= lax.broadcasted_iota(jnp.int32, (128, 128), 1)
    rank = jnp.dot(
        jnp.broadcast_to(flags, (16, 128)).astype(BF), lower.astype(F32).astype(BF), preferred_element_type=F32
    )[0:1]
    slot = lax.broadcasted_iota(jnp.int32, (CAP, 128), 0).astype(F32) + 1.0
    return jnp.where(jnp.logical_and(slot == rank, flags > 0.5), 1.0, 0.0).astype(BF)


def compact_kernel(noised, tokens, cotangent, own):
    pick = selector(noised[...])
    own[0] = jnp.dot(pick, tokens[...], preferred_element_type=F32).astype(BF)
    own[1] = jnp.dot(pick, cotangent[...], preferred_element_type=F32).astype(BF)


def masked(weight, keep, which, model_block, transposed=False):
    rows = []
    for i in range(4):
        cols = []
        for j in range(4):
            f, h = (j, i) if transposed else (i, j)
            flag = keep[which, h, model_block * 4 + f].astype(F32).astype(BF)
            cols.append(weight[i * 128 : (i + 1) * 128, j * 128 : (j + 1) * 128] * flag)
        rows.append(jnp.concatenate(cols, axis=1))
    return jnp.concatenate(rows, axis=0)


def prepare_kernel(
    place, keep, keep_theirs, wg, wu, wd, wg_theirs, wu_theirs,
    gate, up, mine_t, theirs_t, down_t, in_g, in_u, in_d, in_tg, in_tu, sem,
):
    base = place[1] * 4

    def block(i):
        return pl.ds(pl.multiple_of(i * 512, 512), 512)

    def copies(i):
        return [
            pltpu.make_async_copy(wg.at[block(i)], in_g.at[i], sem.at[0, i]),
            pltpu.make_async_copy(wu.at[block(i)], in_u.at[i], sem.at[1, i]),
            pltpu.make_async_copy(wd.at[:, block(i)], in_d.at[i], sem.at[2, i]),
        ]

    def their_copies(i):
        return [
            pltpu.make_async_copy(wg_theirs.at[block(base + i)], in_tg.at[i], sem.at[3, i]),
            pltpu.make_async_copy(wu_theirs.at[block(base + i)], in_tu.at[i], sem.at[4, i]),
        ]

    for i in range(8):
        for copy in copies(i):
            copy.start()
    for i in range(4):
        for copy in their_copies(i):
            copy.start()

    def step(i, carry):
        for copy in copies(i):
            copy.wait()
        gate[i] = masked(in_g.at[i], keep, 0, i)
        up[i] = masked(in_u.at[i], keep, 1, i)
        down_t[i] = masked(in_d.at[i], keep, 2, i, True).T
        return carry

    lax.fori_loop(0, 8, step, 0)

    def their_step(i, carry):
        for copy in their_copies(i):
            copy.wait()
        mine_t[i, 0:512] = gate[base + i].T
        mine_t[i, 512:1024] = up[base + i].T
        theirs_t[i, 0:512] = masked(in_tg.at[i], keep_theirs, 0, base + i).T
        theirs_t[i, 512:1024] = masked(in_tu.at[i], keep_theirs, 1, base + i).T
        return carry

    lax.fori_loop(0, 4, their_step, 0)


def forward_kernel(place, *refs):
    blocks, (gate, up, down_t, ggup, hid_t, xs, cs), scratch = refs[:16], refs[16:23], refs[23:]
    acc_g, acc_u, acc_h = scratch
    x, core, y = place[0], place[1], place[2]
    for other in range(2):
        parity = core ^ other
        for i in range(4):
            own, others = blocks[other * 8 + i], blocks[other * 8 + 4 + i]
            for j in range(4):
                first, second = SHIFTS[j], SHIFTS[i]
                bx = lax.rem(x + 4 - jnp.where(parity == 0, first, second), 4)
                by = lax.rem(y + 4 - jnp.where(parity == 0, second, first), 4)
                r = bx * 2 + parity
                rows = pl.ds(pl.multiple_of(by * CAP, CAP), CAP)
                xs[r, rows] = own[0] if j == 0 else others[j - 1, 0]
                cs[r, rows] = own[1] if j == 0 else others[j - 1, 1]
    acc_g[...] = jnp.zeros_like(acc_g)
    acc_u[...] = jnp.zeros_like(acc_u)
    acc_h[...] = jnp.zeros_like(acc_h)

    def step(r, carry):
        acc_g[...] += jnp.dot(xs[r], gate[r], preferred_element_type=F32)
        acc_u[...] += jnp.dot(xs[r], up[r], preferred_element_type=F32)
        acc_h[...] += jnp.dot(cs[r], down_t[r], preferred_element_type=F32)
        return carry

    lax.fori_loop(0, 8, step, 0)
    g, u, gh = acc_g[...], acc_u[...], acc_h[...]
    sig = 1.0 / (1.0 + jnp.exp(-g))
    silu = g * sig
    ggup[:, 0:512] = (gh * u * sig * (1.0 + g * (1.0 - sig))).astype(BF)
    ggup[:, 512:1024] = (gh * silu).astype(BF)
    hid_t[...] = (silu * u).astype(BF).T


def mine_kernel(mine, mine_t, out):
    def step(q, carry):
        out[q] = jnp.dot(mine[...], mine_t[q], preferred_element_type=F32)
        return carry

    lax.fori_loop(0, 4, step, 0)


def own_kernel(place, part, theirs, theirs_t, o0, o1, o2, o3, full):
    x, core, y = place[0], place[1], place[2]

    def step(q, carry):
        full[q] = part[q] + jnp.dot(theirs[...], theirs_t[q], preferred_element_type=F32)
        return carry

    lax.fori_loop(0, 4, step, 0)
    for shift, out in zip(SHIFTS, (o0, o1, o2, o3)):
        for t in range(4):
            q = jnp.where(core == 0, lax.rem(x + 4 + shift, 4), t)
            c = jnp.where(core == 0, t, lax.rem(y + 4 + shift, 4))
            out[t] = full[q, pl.ds(pl.multiple_of(c * CAP, CAP), CAP)].astype(out.dtype)


def sum_kernel(place, own, r1, r2, r3, o0, o1, o2, o3):
    base = jnp.where(place[1] == 0, place[2], place[0])
    for shift, out in zip(SHIFTS, (o0, o1, o2, o3)):
        t = lax.rem(base + 4 + shift, 4)
        total = own[t] + r1[t].astype(F32) + r2[t].astype(F32) + r3[t].astype(F32)
        out[...] = total.astype(out.dtype)


def expand_kernel(place, noised, t0, t1, t2, t3, u0, u1, u2, u3, out):
    pick = selector(noised[...])
    x, core = place[0], place[1]
    for other, tiles in ((0, (t0, t1, t2, t3)), (1, (u0, u1, u2, u3))):
        for shift, tile in zip(SHIFTS, tiles):
            column = ((core ^ other) * 4 + lax.rem(x + 4 - shift, 4)) * 512
            out[:, pl.ds(pl.multiple_of(column, 512), 512)] = lax.dot_general(
                pick, tile[...], (((0,), (0,)), ((), ())), preferred_element_type=F32
            ).astype(BF)


def gate_up_kernel(keep, xs, ggup, gg, gu, buf_g, buf_u, sem):
    def copies(r):
        rows = pl.ds(pl.multiple_of(r * 512, 512), 512)
        return [
            pltpu.make_async_copy(buf_g.at[r], gg.at[rows], sem.at[0, r]),
            pltpu.make_async_copy(buf_u.at[r], gu.at[rows], sem.at[1, r]),
        ]

    def step(r, carry):
        value = jnp.dot(xs[r].T, ggup[...], preferred_element_type=F32).astype(BF)
        buf_g[r] = masked(value[:, 0:512], keep, 0, r)
        buf_u[r] = masked(value[:, 512:1024], keep, 1, r)
        for copy in copies(r):
            copy.start()
        return carry

    lax.fori_loop(0, 8, step, 0)
    for r in range(8):
        for copy in copies(r):
            copy.wait()


def down_kernel(keep, cs, hid_t, gd, buf, sem):
    def copy(r):
        return pltpu.make_async_copy(buf.at[r], gd.at[:, pl.ds(pl.multiple_of(r * 512, 512), 512)], sem.at[r])

    def step(r, carry):
        value = jnp.dot(hid_t[...], cs[r], preferred_element_type=F32).astype(BF)
        buf[r] = masked(value, keep, 2, r, True)
        copy(r).start()
        return carry

    lax.fori_loop(0, 8, step, 0)
    for r in range(8):
        copy(r).wait()


def shaped(shape, dtype=BF):
    return jax.ShapeDtypeStruct(shape, dtype)


def hbm(array):
    return pltpu.with_memory_space_constraint(array, pltpu.HBM)


def on_device(tokens, cotangent, noised, gate_weight, up_weight, down_weight, block_keep):
    row = lax.axis_index("row")
    place = jnp.stack([row // 2, row % 2, lax.axis_index("col")]).astype(jnp.int32)
    keep = block_keep[0].transpose(0, 2, 1)
    wg, wu, wd = (hbm(w[0]) for w in (gate_weight, up_weight, down_weight))
    rows = 4 * CAP
    barrier = lax.optimization_barrier
    smem = pl.BlockSpec(memory_space=pltpu.SMEM)

    def room(mib):
        return pltpu.CompilerParams(vmem_limit_bytes=mib << 20)

    own = pl.pallas_call(
        compact_kernel, out_shape=shaped((2, CAP, 512)), in_specs=[VM] * 3, out_specs=VM,
        compiler_params=room(4), cost_estimate=cost(5e7, 5e5), name="compact",
    )(*(hbm(v) for v in (noised, tokens[0], cotangent[0])))
    first = [phase(own, 0, SHIFTS[i]) for i in (1, 2, 3)]
    owns = [own] + [phase(own, 1, SHIFTS[i]) for i in (1, 2, 3)]
    next_noised = to_preceding(noised)
    own_theirs = [swap_cores(own)]
    others = jnp.stack(first)
    wg_theirs, wu_theirs = swap_cores(gate_weight), swap_cores(up_weight)
    keep_theirs = swap_cores(block_keep)[0].transpose(0, 2, 1)
    chunks = pltpu.VMEM((8, 512, 512), BF)
    fewer = pltpu.VMEM((4, 512, 512), BF)
    gate, up, mine_t, theirs_t, down_t = pl.pallas_call(
        prepare_kernel,
        out_shape=[shaped((8, 512, 512))] * 2 + [shaped((4, 1024, 512))] * 2 + [shaped((8, 512, 512))],
        in_specs=[smem] * 3 + [ANY] * 5, out_specs=[VM] * 5,
        scratch_shapes=[chunks, chunks, chunks, fewer, fewer, pltpu.SemaphoreType.DMA((5, 8))],
        compiler_params=room(20), cost_estimate=cost(1e7, 3.5e7), name="prepare",
    )(place, keep, keep_theirs, wg, wu, wd, hbm(wg_theirs[0]), hbm(wu_theirs[0]))
    rest = [others] + [phase(others, 1, SHIFTS[i]) for i in (1, 2, 3)]
    own_theirs += [swap_cores(owns[i]) for i in (1, 2, 3)]
    rest_theirs = [swap_cores(rest[i]) for i in range(4)]
    mine, theirs = owns + rest, own_theirs + rest_theirs

    mine[0], next_noised = barrier((mine[0], next_noised))
    ggup, hid_t, xa, ca = pl.pallas_call(
        forward_kernel,
        out_shape=[shaped((rows, 1024)), shaped((512, rows))] + [shaped((8, rows, 512))] * 2,
        in_specs=[smem] + [VM] * 19, out_specs=[VM] * 4,
        scratch_shapes=[pltpu.VMEM((rows, 512), F32)] * 3,
        compiler_params=room(12), cost_estimate=cost(4.8e9, 2.4e7), name="forward",
    )(place, *mine, *theirs, gate, up, down_t)

    ggup_theirs = swap_cores(ggup)
    part = pl.pallas_call(
        mine_kernel, out_shape=shaped((4, rows, 512), F32), in_specs=[VM] * 2, out_specs=VM,
        compiler_params=room(4), cost_estimate=cost(1.6e9, 6e6), name="mine",
    )(ggup, mine_t)
    outs = list(pl.pallas_call(
        own_kernel, out_shape=[shaped((4, CAP, 512), F32)] + [shaped((4, CAP, 512))] * 3,
        in_specs=[smem] + [VM] * 3, out_specs=[VM] * 4,
        scratch_shapes=[pltpu.VMEM((4, rows, 512), F32)],
        compiler_params=room(8), cost_estimate=cost(1.6e9, 1.2e7), name="own",
    )(place, part, ggup_theirs, theirs_t))
    got = [phase(o, 0, d) for o, d in zip(outs[1:], SHIFTS[1:])]
    ggup, outs[0] = barrier((ggup, outs[0]))
    grad_gate, grad_up = pl.pallas_call(
        gate_up_kernel, out_shape=[shaped((4096, 512))] * 2,
        in_specs=[smem] + [VM] * 2, out_specs=[ANY] * 2,
        scratch_shapes=[chunks, chunks, pltpu.SemaphoreType.DMA((2, 8))],
        compiler_params=room(16), cost_estimate=cost(3.2e9, 1.2e7), name="gate_up",
    )(keep, xa, ggup)
    *got, grad_gate, grad_up = barrier((*got, grad_gate, grad_up))
    tiles = pl.pallas_call(
        sum_kernel, out_shape=[shaped((CAP, 512), F32)] + [shaped((CAP, 512))] * 3,
        in_specs=[smem] + [VM] * 4, out_specs=[VM] * 4,
        compiler_params=room(8), cost_estimate=cost(1e6, 2.5e6), name="sum",
    )(place, outs[0], *got)
    got = [phase(o, 1, d) for o, d in zip(tiles[1:], SHIFTS[1:])]
    share = (tiles[0] + sum(g.astype(F32) for g in got)).astype(BF)
    share, hid_t = barrier((share, hid_t))
    share = to_preceding(share)
    grad_down = pl.pallas_call(
        down_kernel, out_shape=shaped((512, 4096)),
        in_specs=[smem] + [VM] * 2, out_specs=ANY,
        scratch_shapes=[chunks, pltpu.SemaphoreType.DMA((8,))],
        compiler_params=room(8), cost_estimate=cost(1.6e9, 8e6), name="down",
    )(keep, ca, hid_t)
    share, grad_down = barrier((share, grad_down))
    strip = [share] + [along_x(share, d) for d in SHIFTS[1:]]
    handoff = pl.pallas_call(
        expand_kernel, out_shape=shaped((128, 4096)),
        in_specs=[smem] + [VM] * 9, out_specs=VM,
        compiler_params=room(8), cost_estimate=cost(1e8, 2e6), name="expand",
    )(place, next_noised, *strip, *[swap_cores(t) for t in strip])
    return (grad_gate[None], grad_up[None], grad_down[None], handoff[None])


def solution(mesh):
    placed = (
        P("section", "col", "row"),
        P("section", "col", "row"),
        P("section", "col"),
        P("section", None, ("row", "col")),
        P("section", None, ("row", "col")),
        P("section", ("row", "col"), None),
        P("section", None, None, ("row", "col")),
    )

    return jax.shard_map(
        on_device,
        mesh=mesh,
        in_specs=placed,
        out_specs=(
            P("section", None, ("row", "col")),
            P("section", None, ("row", "col")),
            P("section", ("row", "col"), None),
            P("section", "col", None),
        ),
        check_vma=False,
    )
```

time: 338 us -> 120 us (0.36)
  waiting for transfers between devices: 196 us -> 25 us
  local copies, waits for them, and re-layouts: 60.7 us -> 2.73 us
  matrix products: 49.1 us -> 0 us
  starting transfers between devices: 3.83 us -> 51.5 us
  Pallas kernels: 0 us -> 39.4 us
  other arithmetic: 13.6 us -> 0.19 us
  between operations: 14.2 us -> 0.87 us
    all_gather x5 -> x0, waiting for transfers between devices: 104 us -> none  [the longest x1 36.9 us: on_device(): lax.all_gather(regroup(wide_cot), 'col', axis=1, tiled=True)]
    reduce_scatter x1 -> x0, waiting for transfers between devices: 91.2 us -> none  [on_device(): lax.psum_scatter(contract_cols(grad_gate_pre, gate_eff) + contract_cols(g...]
    dot_general x8 -> x0, matrix products: 49.1 us -> none  [the longest x3 24.2 us: contract_rows(): lax.dot_general(left, right, (((0,), (0,)), ((), ())), preferred_element_...]
    ppermute x1 -> x36, starting transfers between devices: 3.38 us -> 51.5 us  [the longest x15 24.3 us: phase(): return lax.ppermute(array, ('row', 'col'), pairs)]
    pallas_call x0 -> x9, Pallas kernels: none -> 39.4 us  [the longest x1 9.02 us: on_device(): pl.pallas_call(forward_kernel, out_shape=[shaped((rows, 1024)), shaped((5...]
    unnamed x20 -> x14, local copies, waits for them, and re-layouts: 29.2 us -> 2.73 us
    ppermute x1 -> x36, waiting for transfers between devices: 0.01 us -> 25 us  [the longest x15 17.6 us: phase(): return lax.ppermute(array, ('row', 'col'), pairs)]
    convert_element_type x3 -> x0, local copies, waits for them, and re-layouts: 20.3 us -> none  [expand_blocks(): return widened.astype(jnp.bfloat16)]
  transfers between devices with their start and end apart: 7 -> 36, of which waited for: 5 -> 9; matrix products, arithmetic and copies ran while one was open for 30% -> 0% of each run, Pallas kernels for 0% -> 21%
where the time goes in v1:
time: 120 us
  starting transfers between devices  51.5 us (43%)
  Pallas kernels  39.4 us (33%)
  waiting for transfers between devices  25 us (21%)
  local copies, waits for them, and re-layouts  2.73 us (2%)
    ppermute x15, starting transfers between devices, phase(): return lax.ppermute(array, ('row', 'col'), pairs)  24.3 us
    ppermute x16, starting transfers between devices, swap_cores(): return lax.ppermute(array, 'row', [(i, i ^ 1) for i in range(8)])  20.4 us
    ppermute x15, waiting for transfers between devices, phase(): return lax.ppermute(array, ('row', 'col'), pairs)  17.6 us
    pallas_call x1, Pallas kernels, on_device(): pl.pallas_call(forward_kernel, out_shape=[shaped((rows, 1024)), shaped((5...  9.02 us
    pallas_call x1, Pallas kernels, on_device(): pl.pallas_call(prepare_kernel, out_shape=[shaped((8, 512, 512))] * 2 + [s...  8.41 us
    pallas_call x1, Pallas kernels, on_device(): pl.pallas_call(gate_up_kernel, out_shape=[shaped((4096, 512))] * 2, in_sp...  7.58 us
    ppermute x16, waiting for transfers between devices, swap_cores(): return lax.ppermute(array, 'row', [(i, i ^ 1) for i in range(8)])  7.36 us
    pallas_call x1, Pallas kernels, on_device(): pl.pallas_call(down_kernel, out_shape=shaped((512, 4096)), in_specs=[smem...  5 us
  transfers between devices with their start and end apart: 36, of which 9 were waited for; matrix products, arithmetic and copies ran while one was open for 0% of the time, Pallas kernels for 21%

profile of v1, /device:TPU:97, one launch (start us, length us, event | category | flops | bytes accessed | tf_op | source)
XLA Modules:
  0.0 119.7 jit_solution(2027511736855120926)
XLA Ops:
  1.9 2.0 %collective-permute-start = (s32[1,128]{1,0:T(1,128)}, s32[1,128]{1,0:T(1,128)S(1)}, u32[]{:S(2)}, u32[]{:S(2)}) collective-permute-start(s32[1,128]{1,0:T(1,128)} %noised.1), channel_id=1, source_target_pairs={{32,0},{64,32},{96,64},{33,1},{65,33},{97,65},{34,2},{66,34},{98,6... | collective-permute-start | bytes 1544 | tf_op jit(solution)/shard_map/ppermute | solution.py:41
  3.9 1.3 %compact.1.refs_0_ = bf16[2,96,512]{2,1,0:T(8,128)(2,1)S(1)} custom-call(s32[1,128]{1,0:T(1,128)} %noised.1, bf16[128,512]{1,0:T(8,128)(2,1)} %bitcast.35, bf16[128,512]{1,0:T(8,128)(2,1)} %bitcast.36), custom_call_target="tpu_custom_call" | custom-call | flops 50000000 | bytes 500000 | tf_op jit(solution)/shard_map/compact/pallas_call | solution.py:257
  5.2 1.4 %collective-permute-start.4 = (bf16[2,96,512]{2,1,0:T(8,128)(2,1)S(1)}, bf16[2,96,512]{2,1,0:T(8,128)(2,1)S(1)}, u32[]{:S(2)}, u32[]{:S(2)}) collective-permute-start(bf16[2,96,512]{2,1,0:T(8,128)(2,1)S(1)} %compact.1.refs_0_), channel_id=1, source_target_pairs={{0,8},{1,9},{2,10},{3,11},{4,5},{5,6},{6,7},{7,4},{8,16},{9,17},{1... | collective-permute-start | bytes 589832 | tf_op jit(solution)/shard_map/ppermute | solution.py:29
  6.6 1.5 %collective-permute-start.5 = (bf16[2,96,512]{2,1,0:T(8,128)(2,1)S(1)}, bf16[2,96,512]{2,1,0:T(8,128)(2,1)S(1)}, u32[]{:S(2)}, u32[]{:S(2)}) collective-permute-start(bf16[2,96,512]{2,1,0:T(8,128)(2,1)S(1)} %compact.1.refs_0_), channel_id=1, source_target_pairs={{0,24},{1,25},{2,26},{3,27},{4,7},{5,4},{6,5},{7,6},{8,0},{9,1},{1... | collective-permute-start | bytes 589832 | tf_op jit(solution)/shard_map/ppermute | solution.py:29
  8.1 6.4 %collective-permute-done.18 = s32[1,3,32,4]{2,3,1,0:T(4,128)S(1)} collective-permute-done((s32[1,3,32,4]{2,3,1,0:T(4,128)}, s32[1,3,32,4]{2,3,1,0:T(4,128)S(1)}, u32[]{:S(2)}, u32[]{:S(2)}) %collective-permute-start.18) | collective-permute-done | bytes 1568 | tf_op jit(solution)/shard_map/ppermute | solution.py:33
  14.5 2.9 %collective-permute-start.6 = (bf16[2,96,512]{2,1,0:T(8,128)(2,1)S(1)}, bf16[2,96,512]{2,1,0:T(8,128)(2,1)S(1)}, u32[]{:S(2)}, u32[]{:S(2)}) collective-permute-start(bf16[2,96,512]{2,1,0:T(8,128)(2,1)S(1)} %compact.1.refs_0_), channel_id=1, source_target_pairs={{0,16},{1,17},{2,18},{3,19},{4,6},{5,7},{6,4},{7,5},{8,24},{9,25},... | collective-permute-start | bytes 589832 | tf_op jit(solution)/shard_map/ppermute | solution.py:29
  18.6 1.5 %collective-permute-start.2 = (bf16[2,96,512]{2,1,0:T(8,128)(2,1)S(1)}, bf16[2,96,512]{2,1,0:T(8,128)(2,1)S(1)}, u32[]{:S(2)}, u32[]{:S(2)}) collective-permute-start(bf16[2,96,512]{2,1,0:T(8,128)(2,1)S(1)} %compact.1.refs_0_), channel_id=1, source_target_pairs={{0,3},{1,0},{2,1},{3,2},{4,28},{5,29},{6,30},{7,31},{8,11},{9,8},{... | collective-permute-start | bytes 589832 | tf_op jit(solution)/shard_map/ppermute | solution.py:29
  20.8 3.8 %collective-permute-start.3 = (bf16[2,96,512]{2,1,0:T(8,128)(2,1)S(1)}, bf16[2,96,512]{2,1,0:T(8,128)(2,1)}, u32[]{:S(2)}, u32[]{:S(2)}) collective-permute-start(bf16[2,96,512]{2,1,0:T(8,128)(2,1)S(1)} %compact.1.refs_0_), channel_id=1, source_target_pairs={{0,2},{1,3},{2,0},{3,1},{4,20},{5,21},{6,22},{7,23},{8,10},{9,11},... | collective-permute-start | bytes 589832 | tf_op jit(solution)/shard_map/ppermute | solution.py:29
  24.6 2.7 %collective-permute-start.10 = (bf16[2,96,512]{2,1,0:T(8,128)(2,1)S(1)}, bf16[2,96,512]{2,1,0:T(8,128)(2,1)S(1)}, u32[]{:S(2)}, u32[]{:S(2)}) collective-permute-start(bf16[2,96,512]{2,1,0:T(8,128)(2,1)S(1)} %compact.1.refs_0_), channel_id=1, source_target_pairs={{0,4},{4,0},{8,12},{12,8},{16,20},{20,16},{24,28},{28,24},{1,5},{5... | collective-permute-start | bytes 589832 | tf_op jit(solution)/shard_map/ppermute | solution.py:33
  27.8 3.3 %collective-permute-start.12 = (bf16[2,96,512]{2,1,0:T(8,128)(2,1)S(1)}, bf16[2,96,512]{2,1,0:T(8,128)(2,1)S(1)}, u32[]{:S(2)}, u32[]{:S(2)}) collective-permute-start(bf16[2,96,512]{2,1,0:T(8,128)(2,1)S(1)} %collective-permute-done.2.refs_2_), channel_id=1, source_target_pairs={{0,4},{4,0},{8,12},{12,8},{16,20},{20,16},{24,28},{28,24},{1,5},{5... | collective-permute-start | bytes 589832 | tf_op jit(solution)/shard_map/ppermute | solution.py:33
  33.3 1.8 %collective-permute-start.8 = (bf16[3,2,96,512]{3,2,1,0:T(8,128)(2,1)S(1)}, bf16[3,2,96,512]{3,2,1,0:T(8,128)(2,1)S(1)}, u32[]{:S(2)}, u32[]{:S(2)}) collective-permute-start(bf16[3,2,96,512]{3,2,1,0:T(8,128)(2,1)S(1)} %pad_maximum_fusion.refs_4_), channel_id=1, source_target_pairs={{0,3},{1,0},{2,1},{3,2},{4,28},{5,29},{6,30},{7,31},{8,11},{9,8},{... | collective-permute-start | bytes 1769480 | tf_op jit(solution)/shard_map/ppermute | solution.py:29
  35.8 1.4 %collective-permute-start.9 = (bf16[3,2,96,512]{3,2,1,0:T(8,128)(2,1)S(1)}, bf16[3,2,96,512]{3,2,1,0:T(8,128)(2,1)S(1)}, u32[]{:S(2)}, u32[]{:S(2)}) collective-permute-start(bf16[3,2,96,512]{3,2,1,0:T(8,128)(2,1)S(1)} %pad_maximum_fusion.refs_4_), channel_id=1, source_target_pairs={{0,2},{1,3},{2,0},{3,1},{4,20},{5,21},{6,22},{7,23},{8,10},{9,11},... | collective-permute-start | bytes 1769480 | tf_op jit(solution)/shard_map/ppermute | solution.py:29
  37.2 4.8 %collective-permute-done.7.refs_5_ = bf16[3,2,96,512]{3,2,1,0:T(8,128)(2,1)S(1)} collective-permute-done((bf16[3,2,96,512]{3,2,1,0:T(8,128)(2,1)S(1)}, bf16[3,2,96,512]{3,2,1,0:T(8,128)(2,1)S(1)}, u32[]{:S(2)}, u32[]{:S(2)}) %collective-permute-start.7) | collective-permute-done | bytes 589856 | tf_op jit(solution)/shard_map/ppermute | solution.py:29
  42.9 5.4 %collective-permute-done.8.refs_6_ = bf16[3,2,96,512]{3,2,1,0:T(8,128)(2,1)S(1)} collective-permute-done((bf16[3,2,96,512]{3,2,1,0:T(8,128)(2,1)S(1)}, bf16[3,2,96,512]{3,2,1,0:T(8,128)(2,1)S(1)}, u32[]{:S(2)}, u32[]{:S(2)}) %collective-permute-start.8) | collective-permute-done | bytes 589856 | tf_op jit(solution)/shard_map/ppermute | solution.py:29
  51.3 8.4 %prepare.1 = (bf16[8,512,512]{2,1,0:T(8,128)(2,1)S(1)}, bf16[8,512,512]{2,1,0:T(8,128)(2,1)S(1)}, bf16[4,1024,512]{2,1,0:T(8,128)(2,1)S(1)}, bf16[4,1024,512]{2,1,0:T(8,128)(2,1)S(1)}, bf16[8,512,512]{2,1,0:T(8,128)(2,1)S(1)}) custom-call(s32[3]{0:T(128)S(1)} %pad_add_fusion.place, s32[3,4,32]{2,1,0:T(4,128)S(1)} %bitcast.23, s32[3,4,32]{2,1,0:T(4,128)S(1)} %bitcast.26, ...), custom_call_target="tpu_custom_call" | custom-call | flops 10000000 | bytes 35000000 | tf_op jit(solution)/shard_map/prepare/pallas_call | solution.py:270
  59.8 9.0 %forward.1 = (bf16[384,1024]{1,0:T(8,128)(2,1)S(1)}, bf16[512,384]{1,0:T(8,128)(2,1)S(1)}, bf16[8,384,512]{2,1,0:T(8,128)(2,1)S(1)}, bf16[8,384,512]{2,1,0:T(8,128)(2,1)S(1)}) custom-call(s32[3]{0:T(128)S(1)} %pad_add_fusion.place, bf16[2,96,512]{2,1,0:T(8,128)(2,1)S(1)} %compact.1.refs_0_, bf16[2,96,512]{2,1,0:T(8,128)(2,1)S(1)} %collective-permute-done.1.refs_1_, ...), custom_call_target="tpu_custom_call" | custom-call | flops 4800000000 | bytes 24000000 | tf_op jit(solution)/shard_map/forward/pallas_call | solution.py:283
  69.0 2.3 %mine.1.part = f32[4,384,512]{2,1,0:T(8,128)S(1)} custom-call(bf16[384,1024]{1,0:T(8,128)(2,1)S(1)} %get-tuple-element.48.mine.ggup, bf16[4,1024,512]{2,1,0:T(8,128)(2,1)S(1)} %get-tuple-element.41.mine_t), custom_call_target="tpu_custom_call" | custom-call | flops 1600000000 | bytes 6000000 | tf_op jit(solution)/shard_map/mine/pallas_call | solution.py:292
  71.3 3.0 %own.1 = (f32[4,96,512]{2,1,0:T(8,128)S(1)}, bf16[4,96,512]{2,1,0:T(8,128)(2,1)S(1)}, bf16[4,96,512]{2,1,0:T(8,128)(2,1)S(1)}, bf16[4,96,512]{2,1,0:T(8,128)(2,1)S(1)}) custom-call(s32[3]{0:T(128)S(1)} %pad_add_fusion.place, f32[4,384,512]{2,1,0:T(8,128)S(1)} %mine.1.part, bf16[384,1024]{1,0:T(8,128)(2,1)S(1)} %collective-permute-done.21.theirs, ...), custom_call_target="tpu_custom_call" | custom-call | flops 1600000000 | bytes 12000000 | tf_op jit(solution)/shard_map/own/pallas_call | solution.py:296
  74.3 1.9 %collective-permute-start.22 = (bf16[4,96,512]{2,1,0:T(8,128)(2,1)S(1)}, bf16[4,96,512]{2,1,0:T(8,128)(2,1)S(1)}, u32[]{:S(2)}, u32[]{:S(2)}) collective-permute-start(bf16[4,96,512]{2,1,0:T(8,128)(2,1)S(1)} %get-tuple-element.43), channel_id=1, source_target_pairs={{0,8},{1,9},{2,10},{3,11},{4,5},{5,6},{6,7},{7,4},{8,16},{9,17},{1... | collective-permute-start | bytes 1179656 | tf_op jit(solution)/shard_map/ppermute | solution.py:29
  76.3 1.5 %collective-permute-start.23 = (bf16[4,96,512]{2,1,0:T(8,128)(2,1)S(1)}, bf16[4,96,512]{2,1,0:T(8,128)(2,1)S(1)}, u32[]{:S(2)}, u32[]{:S(2)}) collective-permute-start(bf16[4,96,512]{2,1,0:T(8,128)(2,1)S(1)} %get-tuple-element.44), channel_id=1, source_target_pairs={{0,24},{1,25},{2,26},{3,27},{4,7},{5,4},{6,5},{7,6},{8,0},{9,1},{1... | collective-permute-start | bytes 1179656 | tf_op jit(solution)/shard_map/ppermute | solution.py:29
  78.8 7.6 %gate_up.1 = (bf16[4096,512]{1,0:T(8,128)(2,1)}, bf16[4096,512]{1,0:T(8,128)(2,1)}) custom-call(s32[3,4,32]{2,1,0:T(4,128)S(1)} %bitcast.24, bf16[8,384,512]{2,1,0:T(8,128)(2,1)S(1)} %get-tuple-element.46.xs, bf16[384,1024]{1,0:T(8,128)(2,1)S(1)} %get-tuple-element.48.mine.ggup), custom_call_target="tpu_custom_call" | custom-call | flops 3200000000 | bytes 12000000 | tf_op jit(solution)/shard_map/gate_up/pallas_call | solution.py:304
  86.4 2.1 %collective-permute-done.24.r3 = bf16[4,96,512]{2,1,0:T(8,128)(2,1)S(1)} collective-permute-done((bf16[4,96,512]{2,1,0:T(8,128)(2,1)S(1)}, bf16[4,96,512]{2,1,0:T(8,128)(2,1)S(1)}, u32[]{:S(2)}, u32[]{:S(2)}) %collective-permute-start.24) | collective-permute-done | bytes 393248 | tf_op jit(solution)/shard_map/ppermute | solution.py:29
  89.9 2.0 %collective-permute-start.26 = (bf16[96,512]{1,0:T(8,128)(2,1)S(1)}, bf16[96,512]{1,0:T(8,128)(2,1)S(1)}, u32[]{:S(2)}, u32[]{:S(2)}) collective-permute-start(bf16[96,512]{1,0:T(8,128)(2,1)S(1)} %get-tuple-element.59), channel_id=1, source_target_pairs={{0,3},{1,0},{2,1},{3,2},{4,28},{5,29},{6,30},{7,31},{8,11},{9,8},{... | collective-permute-start | bytes 294920 | tf_op jit(solution)/shard_map/ppermute | solution.py:29
  92.7 1.3 %collective-permute-done.25 = bf16[96,512]{1,0:T(8,128)(2,1)S(1)} collective-permute-done((bf16[96,512]{1,0:T(8,128)(2,1)S(1)}, bf16[96,512]{1,0:T(8,128)(2,1)S(1)}, u32[]{:S(2)}, u32[]{:S(2)}) %collective-permute-start.25) | collective-permute-done | bytes 98336 | tf_op jit(solution)/shard_map/ppermute | solution.py:29
  94.0 3.0 %collective-permute-done.27 = bf16[96,512]{1,0:T(8,128)(2,1)S(1)} collective-permute-done((bf16[96,512]{1,0:T(8,128)(2,1)S(1)}, bf16[96,512]{1,0:T(8,128)(2,1)S(1)}, u32[]{:S(2)}, u32[]{:S(2)}) %collective-permute-start.27) | collective-permute-done | bytes 98336 | tf_op jit(solution)/shard_map/ppermute | solution.py:29
  97.0 2.0 %collective-permute-start.28 = (bf16[96,512]{1,0:T(8,128)(2,1)S(1)}, bf16[96,512]{1,0:T(8,128)(2,1)S(1)}, u32[]{:S(2)}, u32[]{:S(2)}) collective-permute-start(bf16[96,512]{1,0:T(8,128)(2,1)S(1)} %add_convert_fusion), channel_id=1, source_target_pairs={{32,0},{64,32},{96,64},{33,1},{65,33},{97,65},{34,2},{66,34},{98,6... | collective-permute-start | bytes 294920 | tf_op jit(solution)/shard_map/ppermute | solution.py:41
  99.0 5.0 %down.1 = bf16[512,4096]{1,0:T(8,128)(2,1)} custom-call(s32[3,4,32]{2,1,0:T(4,128)S(1)} %bitcast.25, bf16[8,384,512]{2,1,0:T(8,128)(2,1)S(1)} %get-tuple-element.63.cs, bf16[512,384]{1,0:T(8,128)(2,1)S(1)} %get-tuple-element.64.hid_t), custom_call_target="tpu_custom_call" | custom-call | flops 1600000000 | bytes 8000000 | tf_op jit(solution)/shard_map/down/pallas_call | solution.py:320
  104.1 2.7 %collective-permute-start.30 = (bf16[96,512]{1,0:T(8,128)(2,1)S(1)}, bf16[96,512]{1,0:T(8,128)(2,1)S(1)}, u32[]{:S(2)}, u32[]{:S(2)}) collective-permute-start(bf16[96,512]{1,0:T(8,128)(2,1)S(1)} %collective-permute-done.28.t0), channel_id=1, source_target_pairs={{0,24},{4,28},{8,0},{12,4},{16,8},{20,12},{24,16},{28,20},{1,25},{... | collective-permute-start | bytes 294920 | tf_op jit(solution)/shard_map/ppermute | solution.py:37
  106.8 4.1 %collective-permute-start.32 = (bf16[96,512]{1,0:T(8,128)(2,1)S(1)}, bf16[96,512]{1,0:T(8,128)(2,1)S(1)}, u32[]{:S(2)}, u32[]{:S(2)}) collective-permute-start(bf16[96,512]{1,0:T(8,128)(2,1)S(1)} %collective-permute-done.28.t0), channel_id=1, source_target_pairs={{0,4},{4,0},{8,12},{12,8},{16,20},{20,16},{24,28},{28,24},{1,5},{5... | collective-permute-start | bytes 294920 | tf_op jit(solution)/shard_map/ppermute | solution.py:33
  110.9 2.6 %collective-permute-start.33 = (bf16[96,512]{1,0:T(8,128)(2,1)S(1)}, bf16[96,512]{1,0:T(8,128)(2,1)S(1)}, u32[]{:S(2)}, u32[]{:S(2)}) collective-permute-start(bf16[96,512]{1,0:T(8,128)(2,1)S(1)} %collective-permute-done.29.t1), channel_id=1, source_target_pairs={{0,4},{4,0},{8,12},{12,8},{16,20},{20,16},{24,28},{28,24},{1,5},{5... | collective-permute-start | bytes 294920 | tf_op jit(solution)/shard_map/ppermute | solution.py:33
  113.5 3.1 %collective-permute-start.35 = (bf16[96,512]{1,0:T(8,128)(2,1)S(1)}, bf16[96,512]{1,0:T(8,128)(2,1)S(1)}, u32[]{:S(2)}, u32[]{:S(2)}) collective-permute-start(bf16[96,512]{1,0:T(8,128)(2,1)S(1)} %collective-permute-done.31.t3), channel_id=1, source_target_pairs={{0,4},{4,0},{8,12},{12,8},{16,20},{20,16},{24,28},{28,24},{1,5},{5... | collective-permute-start | bytes 294920 | tf_op jit(solution)/shard_map/ppermute | solution.py:33
  117.6 2.1 %expand.1 = bf16[128,4096]{1,0:T(8,128)(2,1)} custom-call(s32[3]{0:T(128)S(1)} %pad_add_fusion.place, s32[1,128]{1,0:T(1,128)S(1)} %collective-permute-done.noised, bf16[96,512]{1,0:T(8,128)(2,1)S(1)} %collective-permute-done.28.t0, bf16[96,512]{1,0:T(8,128)(2,1)S(1)} %collective-permute-done.29.t1, bf16[96,512]{1,0:T(8,128)(2,1)S(1)} %collective-permute-done.30.t2, ...), custom_call_target="tpu_custom_call" | custom-call | flops 100000000 | bytes 2000000 | tf_op jit(solution)/shard_map/expand/pallas_call | solution.py:328
  (66 shorter events, 15.1 us)
Async XLA Ops:
  0.6 49.4 %collective-permute-start.19 = (bf16[1,4096,512]{2,1,0:T(8,128)(2,1)}, bf16[1,4096,512]{2,1,0:T(8,128)(2,1)}, u32[]{:S(2)}, u32[]{:S(2)}) collective-permute-start(bf16[1,4096,512]{2,1,0:T(8,128)(2,1)} %param.10), channel_id=1, source_target_pairs={{0,4},{4,0},{8,12},{12,8},{16,20},{20,16},{24,28},{28,24},{1,5},{5... | collective-permute-start | bytes 12582920 | tf_op jit(solution)/shard_map/ppermute | solution.py:33
  1.4 48.7 %collective-permute-start.20 = (bf16[1,4096,512]{2,1,0:T(8,128)(2,1)}, bf16[1,4096,512]{2,1,0:T(8,128)(2,1)}, u32[]{:S(2)}, u32[]{:S(2)}) collective-permute-start(bf16[1,4096,512]{2,1,0:T(8,128)(2,1)} %param.11), channel_id=1, source_target_pairs={{0,4},{4,0},{8,12},{12,8},{16,20},{20,16},{24,28},{28,24},{1,5},{5... | collective-permute-start | bytes 12582920 | tf_op jit(solution)/shard_map/ppermute | solution.py:33
  1.5 13.0 %collective-permute-start.18 = (s32[1,3,32,4]{2,3,1,0:T(4,128)}, s32[1,3,32,4]{2,3,1,0:T(4,128)S(1)}, u32[]{:S(2)}, u32[]{:S(2)}) collective-permute-start(s32[1,3,32,4]{2,3,1,0:T(4,128)} %param.13), channel_id=1, source_target_pairs={{0,4},{4,0},{8,12},{12,8},{16,20},{20,16},{24,28},{28,24},{1,5},{5... | collective-permute-start | bytes 4616 | tf_op jit(solution)/shard_map/ppermute | solution.py:33
  1.9 4.7 %collective-permute-start = (s32[1,128]{1,0:T(1,128)}, s32[1,128]{1,0:T(1,128)S(1)}, u32[]{:S(2)}, u32[]{:S(2)}) collective-permute-start(s32[1,128]{1,0:T(1,128)} %noised.1), channel_id=1, source_target_pairs={{32,0},{64,32},{96,64},{33,1},{65,33},{97,65},{34,2},{66,34},{98,6... | collective-permute-start | bytes 1544 | tf_op jit(solution)/shard_map/ppermute | solution.py:41
  5.2 12.2 %collective-permute-start.4 = (bf16[2,96,512]{2,1,0:T(8,128)(2,1)S(1)}, bf16[2,96,512]{2,1,0:T(8,128)(2,1)S(1)}, u32[]{:S(2)}, u32[]{:S(2)}) collective-permute-start(bf16[2,96,512]{2,1,0:T(8,128)(2,1)S(1)} %compact.1.refs_0_), channel_id=1, source_target_pairs={{0,8},{1,9},{2,10},{3,11},{4,5},{5,6},{6,7},{7,4},{8,16},{9,17},{1... | collective-permute-start | bytes 589832 | tf_op jit(solution)/shard_map/ppermute | solution.py:29
  6.6 12.0 %collective-permute-start.5 = (bf16[2,96,512]{2,1,0:T(8,128)(2,1)S(1)}, bf16[2,96,512]{2,1,0:T(8,128)(2,1)S(1)}, u32[]{:S(2)}, u32[]{:S(2)}) collective-permute-start(bf16[2,96,512]{2,1,0:T(8,128)(2,1)S(1)} %compact.1.refs_0_), channel_id=1, source_target_pairs={{0,24},{1,25},{2,26},{3,27},{4,7},{5,4},{6,5},{7,6},{8,0},{9,1},{1... | collective-permute-start | bytes 589832 | tf_op jit(solution)/shard_map/ppermute | solution.py:29
  14.5 6.3 %collective-permute-start.6 = (bf16[2,96,512]{2,1,0:T(8,128)(2,1)S(1)}, bf16[2,96,512]{2,1,0:T(8,128)(2,1)S(1)}, u32[]{:S(2)}, u32[]{:S(2)}) collective-permute-start(bf16[2,96,512]{2,1,0:T(8,128)(2,1)S(1)} %compact.1.refs_0_), channel_id=1, source_target_pairs={{0,16},{1,17},{2,18},{3,19},{4,6},{5,7},{6,4},{7,5},{8,24},{9,25},... | collective-permute-start | bytes 589832 | tf_op jit(solution)/shard_map/ppermute | solution.py:29
  17.4 7.2 %collective-permute-start.1 = (bf16[2,96,512]{2,1,0:T(8,128)(2,1)S(1)}, bf16[2,96,512]{2,1,0:T(8,128)(2,1)S(1)}, u32[]{:S(2)}, u32[]{:S(2)}) collective-permute-start(bf16[2,96,512]{2,1,0:T(8,128)(2,1)S(1)} %compact.1.refs_0_), channel_id=1, source_target_pairs={{0,1},{1,2},{2,3},{3,0},{4,12},{5,13},{6,14},{7,15},{8,9},{9,10},{... | collective-permute-start | bytes 589832 | tf_op jit(solution)/shard_map/ppermute | solution.py:29
  18.6 8.6 %collective-permute-start.2 = (bf16[2,96,512]{2,1,0:T(8,128)(2,1)S(1)}, bf16[2,96,512]{2,1,0:T(8,128)(2,1)S(1)}, u32[]{:S(2)}, u32[]{:S(2)}) collective-permute-start(bf16[2,96,512]{2,1,0:T(8,128)(2,1)S(1)} %compact.1.refs_0_), channel_id=1, source_target_pairs={{0,3},{1,0},{2,1},{3,2},{4,28},{5,29},{6,30},{7,31},{8,11},{9,8},{... | collective-permute-start | bytes 589832 | tf_op jit(solution)/shard_map/ppermute | solution.py:29
  20.8 6.9 %collective-permute-start.3 = (bf16[2,96,512]{2,1,0:T(8,128)(2,1)S(1)}, bf16[2,96,512]{2,1,0:T(8,128)(2,1)}, u32[]{:S(2)}, u32[]{:S(2)}) collective-permute-start(bf16[2,96,512]{2,1,0:T(8,128)(2,1)S(1)} %compact.1.refs_0_), channel_id=1, source_target_pairs={{0,2},{1,3},{2,0},{3,1},{4,20},{5,21},{6,22},{7,23},{8,10},{9,11},... | collective-permute-start | bytes 589832 | tf_op jit(solution)/shard_map/ppermute | solution.py:29
  24.6 6.5 %collective-permute-start.10 = (bf16[2,96,512]{2,1,0:T(8,128)(2,1)S(1)}, bf16[2,96,512]{2,1,0:T(8,128)(2,1)S(1)}, u32[]{:S(2)}, u32[]{:S(2)}) collective-permute-start(bf16[2,96,512]{2,1,0:T(8,128)(2,1)S(1)} %compact.1.refs_0_), channel_id=1, source_target_pairs={{0,4},{4,0},{8,12},{12,8},{16,20},{20,16},{24,28},{28,24},{1,5},{5... | collective-permute-start | bytes 589832 | tf_op jit(solution)/shard_map/ppermute | solution.py:33
  27.3 5.4 %collective-permute-start.11 = (bf16[2,96,512]{2,1,0:T(8,128)(2,1)S(1)}, bf16[2,96,512]{2,1,0:T(8,128)(2,1)S(1)}, u32[]{:S(2)}, u32[]{:S(2)}) collective-permute-start(bf16[2,96,512]{2,1,0:T(8,128)(2,1)S(1)} %collective-permute-done.1.refs_1_), channel_id=1, source_target_pairs={{0,4},{4,0},{8,12},{12,8},{16,20},{20,16},{24,28},{28,24},{1,5},{5... | collective-permute-start | bytes 589832 | tf_op jit(solution)/shard_map/ppermute | solution.py:33
  27.8 7.4 %collective-permute-start.12 = (bf16[2,96,512]{2,1,0:T(8,128)(2,1)S(1)}, bf16[2,96,512]{2,1,0:T(8,128)(2,1)S(1)}, u32[]{:S(2)}, u32[]{:S(2)}) collective-permute-start(bf16[2,96,512]{2,1,0:T(8,128)(2,1)S(1)} %collective-permute-done.2.refs_2_), channel_id=1, source_target_pairs={{0,4},{4,0},{8,12},{12,8},{16,20},{20,16},{24,28},{28,24},{1,5},{5... | collective-permute-start | bytes 589832 | tf_op jit(solution)/shard_map/ppermute | solution.py:33
  31.8 10.2 %collective-permute-start.7 = (bf16[3,2,96,512]{3,2,1,0:T(8,128)(2,1)S(1)}, bf16[3,2,96,512]{3,2,1,0:T(8,128)(2,1)S(1)}, u32[]{:S(2)}, u32[]{:S(2)}) collective-permute-start(bf16[3,2,96,512]{3,2,1,0:T(8,128)(2,1)S(1)} %pad_maximum_fusion.refs_4_), channel_id=1, source_target_pairs={{0,1},{1,2},{2,3},{3,0},{4,12},{5,13},{6,14},{7,15},{8,9},{9,10},{... | collective-permute-start | bytes 1769480 | tf_op jit(solution)/shard_map/ppermute | solution.py:29
  33.3 15.0 %collective-permute-start.8 = (bf16[3,2,96,512]{3,2,1,0:T(8,128)(2,1)S(1)}, bf16[3,2,96,512]{3,2,1,0:T(8,128)(2,1)S(1)}, u32[]{:S(2)}, u32[]{:S(2)}) collective-permute-start(bf16[3,2,96,512]{3,2,1,0:T(8,128)(2,1)S(1)} %pad_maximum_fusion.refs_4_), channel_id=1, source_target_pairs={{0,3},{1,0},{2,1},{3,2},{4,28},{5,29},{6,30},{7,31},{8,11},{9,8},{... | collective-permute-start | bytes 1769480 | tf_op jit(solution)/shard_map/ppermute | solution.py:29
  35.8 13.6 %collective-permute-start.9 = (bf16[3,2,96,512]{3,2,1,0:T(8,128)(2,1)S(1)}, bf16[3,2,96,512]{3,2,1,0:T(8,128)(2,1)S(1)}, u32[]{:S(2)}, u32[]{:S(2)}) collective-permute-start(bf16[3,2,96,512]{3,2,1,0:T(8,128)(2,1)S(1)} %pad_maximum_fusion.refs_4_), channel_id=1, source_target_pairs={{0,2},{1,3},{2,0},{3,1},{4,20},{5,21},{6,22},{7,23},{8,10},{9,11},... | collective-permute-start | bytes 1769480 | tf_op jit(solution)/shard_map/ppermute | solution.py:29
  42.0 17.7 %collective-permute-start.14 = (bf16[3,2,96,512]{3,2,1,0:T(8,128)(2,1)S(1)}, bf16[3,2,96,512]{3,2,1,0:T(8,128)(2,1)S(1)}, u32[]{:S(2)}, u32[]{:S(2)}) collective-permute-start(bf16[3,2,96,512]{3,2,1,0:T(8,128)(2,1)S(1)} %pad_maximum_fusion.refs_4_), channel_id=1, source_target_pairs={{0,4},{4,0},{8,12},{12,8},{16,20},{20,16},{24,28},{28,24},{1,5},{5... | collective-permute-start | bytes 1769480 | tf_op jit(solution)/shard_map/ppermute | solution.py:33
  48.3 11.5 %collective-permute-start.15 = (bf16[3,2,96,512]{3,2,1,0:T(8,128)(2,1)S(1)}, bf16[3,2,96,512]{3,2,1,0:T(8,128)(2,1)}, u32[]{:S(2)}, u32[]{:S(2)}) collective-permute-start(bf16[3,2,96,512]{3,2,1,0:T(8,128)(2,1)S(1)} %collective-permute-done.7.refs_5_), channel_id=1, source_target_pairs={{0,4},{4,0},{8,12},{12,8},{16,20},{20,16},{24,28},{28,24},{1,5},{5... | collective-permute-start | bytes 1769480 | tf_op jit(solution)/shard_map/ppermute | solution.py:33
  49.5 10.3 %collective-permute-start.16 = (bf16[3,2,96,512]{3,2,1,0:T(8,128)(2,1)S(1)}, bf16[3,2,96,512]{3,2,1,0:T(8,128)(2,1)}, u32[]{:S(2)}, u32[]{:S(2)}) collective-permute-start(bf16[3,2,96,512]{3,2,1,0:T(8,128)(2,1)S(1)} %collective-permute-done.8.refs_6_), channel_id=1, source_target_pairs={{0,4},{4,0},{8,12},{12,8},{16,20},{20,16},{24,28},{28,24},{1,5},{5... | collective-permute-start | bytes 1769480 | tf_op jit(solution)/shard_map/ppermute | solution.py:33
  50.1 9.8 %collective-permute-start.17 = (bf16[3,2,96,512]{3,2,1,0:T(8,128)(2,1)S(1)}, bf16[3,2,96,512]{3,2,1,0:T(8,128)(2,1)}, u32[]{:S(2)}, u32[]{:S(2)}) collective-permute-start(bf16[3,2,96,512]{3,2,1,0:T(8,128)(2,1)S(1)} %collective-permute-done.9.refs_7_), channel_id=1, source_target_pairs={{0,4},{4,0},{8,12},{12,8},{16,20},{20,16},{24,28},{28,24},{1,5},{5... | collective-permute-start | bytes 1769480 | tf_op jit(solution)/shard_map/ppermute | solution.py:33
  50.1 9.7 %collective-permute-start.13 = (bf16[2,96,512]{2,1,0:T(8,128)(2,1)}, bf16[2,96,512]{2,1,0:T(8,128)(2,1)}, u32[]{:S(2)}, u32[]{:S(2)}) collective-permute-start(bf16[2,96,512]{2,1,0:T(8,128)(2,1)} %collective-permute-done.3.refs_3_), channel_id=1, source_target_pairs={{0,4},{4,0},{8,12},{12,8},{16,20},{20,16},{24,28},{28,24},{1,5},{5... | collective-permute-start | bytes 589832 | tf_op jit(solution)/shard_map/ppermute | solution.py:33
  74.3 12.1 %collective-permute-start.22 = (bf16[4,96,512]{2,1,0:T(8,128)(2,1)S(1)}, bf16[4,96,512]{2,1,0:T(8,128)(2,1)S(1)}, u32[]{:S(2)}, u32[]{:S(2)}) collective-permute-start(bf16[4,96,512]{2,1,0:T(8,128)(2,1)S(1)} %get-tuple-element.43), channel_id=1, source_target_pairs={{0,8},{1,9},{2,10},{3,11},{4,5},{5,6},{6,7},{7,4},{8,16},{9,17},{1... | collective-permute-start | bytes 1179656 | tf_op jit(solution)/shard_map/ppermute | solution.py:29
  76.3 10.2 %collective-permute-start.23 = (bf16[4,96,512]{2,1,0:T(8,128)(2,1)S(1)}, bf16[4,96,512]{2,1,0:T(8,128)(2,1)S(1)}, u32[]{:S(2)}, u32[]{:S(2)}) collective-permute-start(bf16[4,96,512]{2,1,0:T(8,128)(2,1)S(1)} %get-tuple-element.44), channel_id=1, source_target_pairs={{0,24},{1,25},{2,26},{3,27},{4,7},{5,4},{6,5},{7,6},{8,0},{9,1},{1... | collective-permute-start | bytes 1179656 | tf_op jit(solution)/shard_map/ppermute | solution.py:29
  77.7 10.8 %collective-permute-start.24 = (bf16[4,96,512]{2,1,0:T(8,128)(2,1)S(1)}, bf16[4,96,512]{2,1,0:T(8,128)(2,1)S(1)}, u32[]{:S(2)}, u32[]{:S(2)}) collective-permute-start(bf16[4,96,512]{2,1,0:T(8,128)(2,1)S(1)} %get-tuple-element.45), channel_id=1, source_target_pairs={{0,16},{1,17},{2,18},{3,19},{4,6},{5,7},{6,4},{7,5},{8,24},{9,25},... | collective-permute-start | bytes 1179656 | tf_op jit(solution)/shard_map/ppermute | solution.py:29
  89.2 4.7 %collective-permute-start.25 = (bf16[96,512]{1,0:T(8,128)(2,1)S(1)}, bf16[96,512]{1,0:T(8,128)(2,1)S(1)}, u32[]{:S(2)}, u32[]{:S(2)}) collective-permute-start(bf16[96,512]{1,0:T(8,128)(2,1)S(1)} %get-tuple-element.58), channel_id=1, source_target_pairs={{0,1},{1,2},{2,3},{3,0},{4,12},{5,13},{6,14},{7,15},{8,9},{9,10},{... | collective-permute-start | bytes 294920 | tf_op jit(solution)/shard_map/ppermute | solution.py:29
  92.0 5.0 %collective-permute-start.27 = (bf16[96,512]{1,0:T(8,128)(2,1)S(1)}, bf16[96,512]{1,0:T(8,128)(2,1)S(1)}, u32[]{:S(2)}, u32[]{:S(2)}) collective-permute-start(bf16[96,512]{1,0:T(8,128)(2,1)S(1)} %get-tuple-element.60), channel_id=1, source_target_pairs={{0,2},{1,3},{2,0},{3,1},{4,20},{5,21},{6,22},{7,23},{8,10},{9,11},... | collective-permute-start | bytes 294920 | tf_op jit(solution)/shard_map/ppermute | solution.py:29
  97.0 7.0 %collective-permute-start.28 = (bf16[96,512]{1,0:T(8,128)(2,1)S(1)}, bf16[96,512]{1,0:T(8,128)(2,1)S(1)}, u32[]{:S(2)}, u32[]{:S(2)}) collective-permute-start(bf16[96,512]{1,0:T(8,128)(2,1)S(1)} %add_convert_fusion), channel_id=1, source_target_pairs={{32,0},{64,32},{96,64},{33,1},{65,33},{97,65},{34,2},{66,34},{98,6... | collective-permute-start | bytes 294920 | tf_op jit(solution)/shard_map/ppermute | solution.py:41
  104.0 6.8 %collective-permute-start.29 = (bf16[96,512]{1,0:T(8,128)(2,1)S(1)}, bf16[96,512]{1,0:T(8,128)(2,1)S(1)}, u32[]{:S(2)}, u32[]{:S(2)}) collective-permute-start(bf16[96,512]{1,0:T(8,128)(2,1)S(1)} %collective-permute-done.28.t0), channel_id=1, source_target_pairs={{0,8},{4,12},{8,16},{12,20},{16,24},{20,28},{24,0},{28,4},{1,9},{5... | collective-permute-start | bytes 294920 | tf_op jit(solution)/shard_map/ppermute | solution.py:37
  104.1 9.4 %collective-permute-start.30 = (bf16[96,512]{1,0:T(8,128)(2,1)S(1)}, bf16[96,512]{1,0:T(8,128)(2,1)S(1)}, u32[]{:S(2)}, u32[]{:S(2)}) collective-permute-start(bf16[96,512]{1,0:T(8,128)(2,1)S(1)} %collective-permute-done.28.t0), channel_id=1, source_target_pairs={{0,24},{4,28},{8,0},{12,4},{16,8},{20,12},{24,16},{28,20},{1,25},{... | collective-permute-start | bytes 294920 | tf_op jit(solution)/shard_map/ppermute | solution.py:37
  106.8 6.7 %collective-permute-start.31 = (bf16[96,512]{1,0:T(8,128)(2,1)S(1)}, bf16[96,512]{1,0:T(8,128)(2,1)S(1)}, u32[]{:S(2)}, u32[]{:S(2)}) collective-permute-start(bf16[96,512]{1,0:T(8,128)(2,1)S(1)} %collective-permute-done.28.t0), channel_id=1, source_target_pairs={{0,16},{4,20},{8,24},{12,28},{16,0},{20,4},{24,8},{28,12},{1,17},{... | collective-permute-start | bytes 294920 | tf_op jit(solution)/shard_map/ppermute | solution.py:37
  106.8 9.9 %collective-permute-start.32 = (bf16[96,512]{1,0:T(8,128)(2,1)S(1)}, bf16[96,512]{1,0:T(8,128)(2,1)S(1)}, u32[]{:S(2)}, u32[]{:S(2)}) collective-permute-start(bf16[96,512]{1,0:T(8,128)(2,1)S(1)} %collective-permute-done.28.t0), channel_id=1, source_target_pairs={{0,4},{4,0},{8,12},{12,8},{16,20},{20,16},{24,28},{28,24},{1,5},{5... | collective-permute-start | bytes 294920 | tf_op jit(solution)/shard_map/ppermute | solution.py:33
  110.9 5.8 %collective-permute-start.33 = (bf16[96,512]{1,0:T(8,128)(2,1)S(1)}, bf16[96,512]{1,0:T(8,128)(2,1)S(1)}, u32[]{:S(2)}, u32[]{:S(2)}) collective-permute-start(bf16[96,512]{1,0:T(8,128)(2,1)S(1)} %collective-permute-done.29.t1), channel_id=1, source_target_pairs={{0,4},{4,0},{8,12},{12,8},{16,20},{20,16},{24,28},{28,24},{1,5},{5... | collective-permute-start | bytes 294920 | tf_op jit(solution)/shard_map/ppermute | solution.py:33
  (11 other events, 41.9 us)
